TPU v7x, 128 devices: a whole 4x4x4 slice. The times are simulated.
128 devices in a mesh: req: 16 (over z, y), kv: 8 (over x, core).
Axes of the slice: x: 4, y: 4, z: 4, core: 2. Of those that a mesh axis runs over, the one named last changes fastest.
Arguments:
- hidden_in: bfloat16 [16384, 2048], P(('req', 'kv')), may hold values from -6 to 6
- slot_tokens: int32 [16384], replicated, may hold values from 0 to 16383, as said below
- cache_len: int32 [128], P('req'), may hold values from 1 to 2048, 65536 in all
- prefill_start: int32 [16], P('req'), may hold values from 0 to 2048
- key_cache: bfloat16 [128, 2048, 1024], P('req', None, 'kv')
- value_cache: bfloat16 [128, 2048, 1024], P('req', None, 'kv'), may hold values from -18 to 18
- key_prefix: bfloat16 [16, 2048, 1024], P('req', None, 'kv')
- value_prefix: bfloat16 [16, 2048, 1024], P('req', None, 'kv'), may hold values from -18 to 18
- attn_gain: float32 [2048], replicated, may hold values from 0.25 to 1.75
- q_proj: bfloat16 [2048, 2048], P(None, 'kv'), may hold values from -0.125 to 0.125
- k_proj: bfloat16 [2048, 1024], P(None, 'kv'), may hold values from -0.125 to 0.125
- v_proj: bfloat16 [2048, 1024], P(None, 'kv'), may hold values from -0.125 to 0.125
- q_gain: float32 [128], replicated, may hold values from 0.25 to 1.75
- k_gain: float32 [128], replicated, may hold values from 0.25 to 1.75
- o_proj: bfloat16 [2048, 2048], P('kv'), may hold values from -0.125 to 0.125
- ffn_gain: float32 [2048], replicated, may hold values from 0.25 to 1.75
- w_gate: bfloat16 [2048, 6144], P(None, 'req'), may hold values from -0.125 to 0.125
- w_up: bfloat16 [2048, 6144], P(None, 'req'), may hold values from -0.125 to 0.125
- w_down: bfloat16 [6144, 2048], P('req'), may hold values from -0.078125 to 0.078125
- final_gain: float32 [2048], replicated, may hold values from 0.25 to 1.75
- lm_head: bfloat16 [2048, 151936], P(None, ('req', 'kv')), may hold values from -0.375 to 0.375
Outputs:
- layer_out: bfloat16 [16384, 2048], P(('req', 'kv'))
- max_logit: float32 [144], replicated
Inputs may be any that keep to these rules, and one draw needn't show every extreme that they name: slot_tokens is a permutation of the batch's tokens; each device's 128 consecutive slots take exactly 1 token from each device's 128 consecutive batch tokens.
All inputs are finite; a program needn't handle non-finite values. No bound on the sum of `cache_len` on one device may be relied on, other than what follows from the above.
Results may differ from a plain program's by a relative error of at most 0.0085.
The roundings to bfloat16 on the way count: a program that leaves them out, or rounds other values in their place, can miss the bound.
Values may be sent and summed in bfloat16 or wider, within the bound.
A program may use at most 128 MiB of HBM per device.

v0:
```python
import jax
import jax.numpy as jnp
from jax import lax
from jax.sharding import PartitionSpec as P

EPS = 1e-06
NEG = -1e30


def spread(value, axis, root):
    mine = lax.axis_index(axis) == root
    return lax.psum(jnp.where(mine, value, jnp.zeros_like(value)), axis)


def norm_rows(values, gain_vec):
    wide = values.astype(jnp.float32)
    return wide * lax.rsqrt(jnp.mean(wide * wide, axis=-1, keepdims=True) + EPS) * gain_vec


def rotate(values, places):
    half_dim = values.shape[-1] // 2
    freqs = 1000000.0 ** (-(jnp.arange(half_dim, dtype=jnp.float32) * 2.0 / values.shape[-1]))
    angles = places[:, None] * freqs[None, :]
    cosine = jnp.cos(angles)[:, None, :]
    sine = jnp.sin(angles)[:, None, :]
    first_half = values[..., :half_dim]
    second_half = values[..., half_dim:]
    return jnp.concatenate(
        [first_half * cosine - second_half * sine, second_half * cosine + first_half * sine],
        axis=-1,
    )


def prefill_full(q_heads, key_old, value_old, key_new, value_new, start_at):
    old_len = key_old.shape[0]
    fresh_rows = q_heads.shape[0]
    factor = q_heads.shape[-1] ** (-0.5)
    all_keys = jnp.concatenate([key_old, key_new], axis=0)
    all_values = jnp.concatenate([value_old, value_new], axis=0)
    scores = (
        jnp.einsum("cgd,kd->gck", q_heads, all_keys, preferred_element_type=jnp.float32) * factor
    )
    key_index = jnp.arange(old_len + fresh_rows, dtype=jnp.int32)[None, :]
    row_index = jnp.arange(fresh_rows, dtype=jnp.int32)[:, None]
    allowed = jnp.where(key_index < old_len, key_index < start_at, key_index - old_len <= row_index)
    scores = jnp.where(allowed[None], scores, NEG)
    row_peak = jnp.max(scores, axis=-1, keepdims=True)
    expd = jnp.exp(scores - row_peak)
    weights = (expd / jnp.sum(expd, axis=-1, keepdims=True)).astype(jnp.bfloat16)
    return jnp.einsum(
        "gck,kd->cgd", weights, all_values, preferred_element_type=jnp.float32
    ).astype(jnp.bfloat16)


def decode_attend(q_heads, key_old, value_old, key_self, value_self, lengths):
    factor = q_heads.shape[-1] ** (-0.5)
    past = jnp.einsum("bgd,bld->bgl", q_heads, key_old, preferred_element_type=jnp.float32) * factor
    slot_index = jnp.arange(key_old.shape[1], dtype=jnp.int32)
    past = jnp.where(slot_index[None, None, :] < lengths[:, None, None], past, NEG)
    own_score = (
        jnp.einsum("bgd,bd->bg", q_heads, key_self, preferred_element_type=jnp.float32) * factor
    )
    row_peak = jnp.maximum(jnp.max(past, axis=-1), own_score)
    past_exp = jnp.exp(past - row_peak[..., None])
    own_exp = jnp.exp(own_score - row_peak)
    row_total = jnp.sum(past_exp, axis=-1) + own_exp
    past_w = (past_exp / row_total[..., None]).astype(jnp.bfloat16)
    own_w = (own_exp / row_total).astype(jnp.bfloat16)
    summed = jnp.einsum("bgl,bld->bgd", past_w, value_old, preferred_element_type=jnp.float32)
    summed = (
        summed + own_w.astype(jnp.float32)[..., None] * value_self.astype(jnp.float32)[:, None, :]
    )
    return summed.astype(jnp.bfloat16)


def regroup(rows_in):
    return lax.all_to_all(rows_in, ("req", "kv"), split_axis=0, concat_axis=0, tiled=True)


def shards(
    hidden_in,
    slot_tokens,
    cache_len,
    prefill_start,
    key_cache,
    value_cache,
    key_prefix,
    value_prefix,
    attn_gain,
    q_proj,
    k_proj,
    v_proj,
    q_gain,
    k_gain,
    o_proj,
    ffn_gain,
    w_gate,
    w_up,
    w_down,
    final_gain,
    lm_head,
):
    req_count = lax.axis_size("req")
    kv_count = lax.axis_size("kv")
    devices = req_count * kv_count
    rows_dev = hidden_in.shape[0]
    per_pair = rows_dev // devices
    self_index = lax.axis_index("req") * kv_count + lax.axis_index("kv")
    slot_table = slot_tokens.reshape(devices, rows_dev)
    from_self = slot_table // rows_dev == self_index
    picked = jnp.argsort(jnp.where(from_self, 0, 1).astype(jnp.int32), axis=1, stable=True)[
        :, :per_pair
    ]
    send_rows = (jnp.take_along_axis(slot_table, picked, axis=1) - self_index * rows_dev).reshape(
        -1
    )
    own_sources = lax.dynamic_index_in_dim(slot_table, self_index, 0, keepdims=False) // rows_dev
    marks = (own_sources[:, None] == jnp.arange(devices, dtype=jnp.int32)[None, :]).astype(
        jnp.int32
    )
    ranks = jnp.sum(marks * (jnp.cumsum(marks, axis=0) - 1), axis=1)
    slot_place = own_sources * per_pair + ranks
    arrived = regroup(hidden_in[send_rows])
    owner_rows = arrived[slot_place]
    normed = norm_rows(owner_rows, attn_gain).astype(jnp.bfloat16)
    q_cols = q_proj.shape[1]
    kv_cols = k_proj.shape[1]
    rows_piece = lax.all_gather(normed, "kv", axis=0, tiled=True)
    projected = jnp.concatenate(
        [
            jnp.dot(rows_piece, q_proj, preferred_element_type=jnp.float32),
            jnp.dot(rows_piece, k_proj, preferred_element_type=jnp.float32),
            jnp.dot(rows_piece, v_proj, preferred_element_type=jnp.float32),
        ],
        axis=1,
    )
    tok_req = projected.shape[0]
    head_dim = q_gain.shape[0]
    dec_count = cache_len.shape[0]
    fresh_count = tok_req - dec_count
    q_raw = projected[:, :q_cols].reshape(tok_req, q_cols // head_dim, head_dim)
    k_raw = projected[:, q_cols : q_cols + kv_cols].reshape(tok_req, kv_cols // head_dim, head_dim)
    v_new = (
        projected[:, q_cols + kv_cols :]
        .astype(jnp.bfloat16)
        .reshape(tok_req, kv_cols // head_dim, head_dim)
    )
    places = jnp.concatenate(
        [prefill_start[0] + jnp.arange(fresh_count, dtype=jnp.int32), cache_len]
    ).astype(jnp.float32)
    queries = rotate(norm_rows(q_raw, q_gain), places).astype(jnp.bfloat16)
    keys_new = rotate(norm_rows(k_raw, k_gain), places).astype(jnp.bfloat16)
    pre_out = prefill_full(
        queries[:fresh_count],
        key_prefix[0, :, 0:head_dim],
        value_prefix[0, :, 0:head_dim],
        keys_new[:fresh_count, 0],
        v_new[:fresh_count, 0],
        prefill_start[0],
    )
    dec_out = decode_attend(
        queries[fresh_count:],
        key_cache,
        value_cache,
        keys_new[fresh_count:, 0],
        v_new[fresh_count:, 0],
        cache_len,
    )
    pieces = jnp.concatenate([pre_out, dec_out], axis=0)
    attended = pieces.reshape(tok_req, q_cols)
    attn_part = lax.psum_scatter(
        jnp.dot(attended, o_proj, preferred_element_type=jnp.float32),
        "kv",
        scatter_dimension=0,
        tiled=True,
    )
    resid = (owner_rows.astype(jnp.float32) + attn_part).astype(jnp.bfloat16)
    ffn_in = norm_rows(resid, ffn_gain).astype(jnp.bfloat16)
    rows_piece = lax.all_gather(ffn_in, "req", axis=0, tiled=True)
    gate_part = jnp.dot(rows_piece, w_gate, preferred_element_type=jnp.float32)
    up_part = jnp.dot(rows_piece, w_up, preferred_element_type=jnp.float32)
    hidden_act = (jax.nn.silu(gate_part) * up_part).astype(jnp.bfloat16)
    ffn_part = lax.psum_scatter(
        jnp.dot(hidden_act, w_down, preferred_element_type=jnp.float32),
        "req",
        scatter_dimension=0,
        tiled=True,
    )
    out_rows = (resid.astype(jnp.float32) + ffn_part).astype(jnp.bfloat16)
    going_back = jnp.zeros_like(out_rows).at[slot_place].set(out_rows)
    returned = regroup(going_back)
    layer_out = jnp.zeros_like(hidden_in).at[send_rows].set(returned)
    tail_rows = norm_rows(out_rows[rows_dev - dec_count - 1 :], final_gain).astype(jnp.bfloat16)
    tail_rows = spread(tail_rows, "kv", kv_count - 1)
    local_peaks = jnp.max(
        jnp.dot(
            lax.all_gather(tail_rows, "req", axis=0, tiled=True),
            lm_head,
            preferred_element_type=jnp.float32,
        ),
        axis=1,
    )
    max_logit = lax.pmax(local_peaks, ("req", "kv"))
    return (layer_out, max_logit)


def solution(mesh):
    placed = (
        P(("req", "kv"), None),
        P(),
        P("req"),
        P("req"),
        P("req", None, "kv"),
        P("req", None, "kv"),
        P("req", None, "kv"),
        P("req", None, "kv"),
        P(),
        P(None, "kv"),
        P(None, "kv"),
        P(None, "kv"),
        P(),
        P(),
        P("kv", None),
        P(),
        P(None, "req"),
        P(None, "req"),
        P("req", None),
        P(),
        P(None, ("req", "kv")),
    )
    return jax.shard_map(
        shards, mesh=mesh, in_specs=placed, out_specs=(P(("req", "kv"), None), P()), check_vma=False
    )
```

profile of v0, /device:TPU:1, one launch (start us, length us, event | category | flops | bytes accessed | tf_op | source)
XLA Modules:
  0.0 540.3 jit_solution(2482450521483599496)
XLA Ops:
  11.1 4.7 sort.19.cloned.1.call-done
  17.0 1.9 gather_fusion.2
  23.6 11.5 %all-to-all-start = ((bf16[128,2,1024]{2,1,0:T(2,128)(2,1)}), bf16[128,2,1024]{2,1,0:T(2,128)(2,1)S(1)}, u32[]{:S(2)}, u32[]{:S(2)}) async-start(bf16[128,2,1024]{2,1,0:T(2,128)(2,1)} %reshape.484), calls=%async_computation | async-start | bytes 1048576 | tf_op jit(solution)/shard_map/all_to_all | solution.py:77
  35.9 13.0 %all-to-all-done = bf16[128,2,1024]{2,1,0:T(2,128)(2,1)S(1)} async-done(((bf16[128,2,1024]{2,1,0:T(2,128)(2,1)}), bf16[128,2,1024]{2,1,0:T(2,128)(2,1)S(1)}, u32[]{:S(2)}, u32[]{:S(2)}) %all-to-all-start) | async-done | bytes 524320 | tf_op jit(solution)/shard_map/all_to_all | solution.py:77
  55.4 3.1 multiply_cosine_fusion
  58.6 4.2 fusion.4
  62.7 20.4 %all-gather.4.cloned.1.call-done = bf16[1024,2048]{1,0:T(8,128)(2,1)} async-done(((bf16[128,2048]{1,0:T(8,128)(2,1)}), bf16[1024,2048]{1,0:T(8,128)(2,1)}) %all-gather.4.cloned.1.call-update) | async-done | bytes 4194320 | tf_op jit(solution)/shard_map/all_gather | solution.py:128
  83.2 3.6 convolution_convert_fusion
  90.5 2.3 multiply_reduce_fusion
  99.4 2.9 fusion.43
  102.4 15.9 %fusion.84 = (f32[2,1016]{1,0:T(2,128)S(1)}, f32[2,1016,3064]{2,1,0:T(8,128)}) fusion(pred[1016,3064]{1,0:T(8,128)(4,1)} %fusion.4, bf16[1016,128]{1,0:T(8,128)(2,1)} %copy.80, bf16[2048,128]{1,0:T(8,128)(2,1)} %bitcast.105, bf16[1024,2,64]{2,0,1:T(8,128)(2,1)S(1)} %get-tuple-element.6, bf16[1024,2,64]{2,0,1:T(8,128)(2,1)S(1)} %get-tuple-element.7), kind=kOutput, calls=%fused_computation.161 | convolution fusion | flops 1621384704 | bytes 29334016 | tf_op jit(solution)/shard_map/sub | solution.py:48
  118.3 11.7 %fusion.12 = bf16[1016,2,128]{2,0,1:T(8,128)(2,1)S(1)} fusion(f32[2,1016,3064]{2,1,0:T(8,128)} %get-tuple-element.21, f32[2,1016]{1,0:T(2,128)S(1)} %get-tuple-element.20, bf16[1016,128]{1,0:T(8,128)(2,1)S(1)} %copy-done.5, bf16[2048,128]{1,0:T(8,128)(2,1)} %bitcast.106), kind=kOutput, calls=%fused_computation.28 | convolution fusion | flops 1608149248 | bytes 26216896 | tf_op jit(solution)/shard_map/gck,kd->cgd/dot_general | solution.py:50
  130.3 5.7 %fusion.89 = f32[1024,2048]{1,0:T(8,128)} fusion(bf16[1024,256]{0,1:T(8,128)(2,1)S(1)} %bitcast.94, bf16[256,2048]{1,0:T(8,128)(2,1)} %param.35), kind=kOutput, calls=%fused_computation.162 | convolution fusion | flops 1073741824 | bytes 9961472 | tf_op jit(solution)/shard_map/dot_general | solution.py:172
  136.1 51.5 %reduce-scatter.3.cloned.1.call-done = f32[128,2048]{1,0:T(8,128)} async-done(((f32[1024,2048]{1,0:T(8,128)}), f32[128,2048]{1,0:T(8,128)}) %reduce-scatter.3.cloned.1.call-update) | async-done | bytes 1048592 | tf_op jit(solution)/shard_map/reduce_scatter | solution.py:171
  190.4 71.2 %all-gather.6.cloned.1.call-done = bf16[2048,2048]{1,0:T(8,128)(2,1)} async-done(((bf16[128,2048]{1,0:T(8,128)(2,1)}), bf16[2048,2048]{1,0:T(8,128)(2,1)}) %all-gather.6.cloned.1.call-update) | async-done | bytes 8388624 | tf_op jit(solution)/shard_map/all_gather | solution.py:179
  261.5 10.1 %fusion.90 = f32[2048,384]{1,0:T(8,128)} fusion(bf16[2048,2048]{1,0:T(8,128)(2,1)} %all-gather.6.cloned.1.call-done, bf16[2048,384]{1,0:T(8,128)(2,1)} %param.37), kind=kOutput, calls=%fused_computation.163 | convolution fusion | flops 3221225472 | bytes 13107200 | tf_op jit(solution)/shard_map/dot_general | solution.py:180
  271.6 15.4 %fusion.10 = f32[2048,2048]{1,0:T(8,128)} fusion(bf16[384,2048]{1,0:T(8,128)(2,1)S(1)} %copy-done, f32[2048,384]{1,0:T(8,128)} %fusion.90, bf16[2048,2048]{1,0:T(8,128)(2,1)} %all-gather.6.cloned.1.call-done, bf16[2048,384]{1,0:T(8,128)(2,1)} %param.38), kind=kOutput, calls=%fused_computation.26 | convolution fusion | flops 6447169536 | bytes 31457280 | tf_op jit(solution)/shard_map/dot_general | solution.py:184
  287.0 110.1 %reduce-scatter.5.cloned.1.call-done = f32[128,2048]{1,0:T(8,128)} async-done(((f32[2048,2048]{1,0:T(8,128)}), f32[128,2048]{1,0:T(8,128)}) %reduce-scatter.5.cloned.1.call-update) | async-done | bytes 1048592 | tf_op jit(solution)/shard_map/reduce_scatter | solution.py:183
  402.4 23.1 %psum.7 = bf16[9,2048]{1,0:T(8,128)(2,1)S(1)} all-reduce(bf16[9,2048]{1,0:T(8,128)(2,1)S(1)} %fusion.48), channel_id=1, replica_groups=mesh['req'=16,'kv'=8] {'kv'}, use_global_device_ids=true, to_apply=%region_16.17 | all-reduce | flops 18432 | bytes 73728 | tf_op jit(solution)/shard_map/psum | solution.py:12
  425.5 8.6 %all-to-all-start.1 = ((bf16[128,2,1024]{2,1,0:T(2,128)(2,1)}), bf16[128,2,1024]{2,1,0:T(2,128)(2,1)S(1)}, u32[]{:S(2)}, u32[]{:S(2)}) async-start(bf16[128,2,1024]{2,1,0:T(2,128)(2,1)} %reshape.486), calls=%async_computation.3 | async-start | bytes 1048576 | tf_op jit(solution)/shard_map/all_to_all | solution.py:77
  434.1 22.4 %all-gather = bf16[16,9,2048]{2,1,0:T(8,128)(2,1)S(1)} all-gather(bf16[1,9,2048]{2,1,0:T(8,128)(2,1)S(1)} %bitcast.99), channel_id=1, replica_groups=mesh['req'=16,'kv'=8] {'req'}, dimensions={0}, use_global_device_ids=true | all-gather | bytes 626688 | tf_op jit(solution)/shard_map/all_gather | solution.py:197
  457.5 4.4 convolution_reduce_fusion
  461.9 68.8 %pmax.7 = f32[144]{0:T(256)} all-reduce(f32[144]{0:T(256)S(1)} %convolution_reduce_fusion), channel_id=1, replica_groups=mesh['req'=16,'kv'=8] {'req','kv'}, use_global_device_ids=true, to_apply=%region_18.19 | all-reduce | flops 144 | bytes 1152 | tf_op jit(solution)/shard_map/pmax | solution.py:203
  531.1 2.4 scatter_custom_fusion.1
  (110 shorter events, 36.5 us)
Async XLA Ops:
  7.2 264.4 %copy-start = (bf16[384,2048]{1,0:T(8,128)(2,1)S(1)}, bf16[384,2048]{1,0:T(8,128)(2,1)}, u32[]{:S(2)}) copy-start(bf16[384,2048]{1,0:T(8,128)(2,1)} %param.39) | copy-start | bytes 4718596
  7.2 12.8 %copy-start.1 = (bf16[128,2048]{1,0:T(8,128)(2,1)S(1)}, bf16[128,2048]{1,0:T(8,128)(2,1)}, u32[]{:S(2)}) copy-start(bf16[128,2048]{1,0:T(8,128)(2,1)} %param.21) | copy-start | bytes 1572868
  7.2 8.5 %sort.19.cloned.1.call-start = ((), (), s32[]{:S(2)}) async-start(), calls=%async_computation.8 | async-start | bytes 393248 | tf_op jit(solution)/shard_map/jit(argsort)/sort | solution.py:111
  23.6 25.2 %all-to-all-start = ((bf16[128,2,1024]{2,1,0:T(2,128)(2,1)}), bf16[128,2,1024]{2,1,0:T(2,128)(2,1)S(1)}, u32[]{:S(2)}, u32[]{:S(2)}) async-start(bf16[128,2,1024]{2,1,0:T(2,128)(2,1)} %reshape.484), calls=%async_computation | async-start | bytes 1048576 | tf_op jit(solution)/shard_map/all_to_all | solution.py:77
  35.1 48.0 %all-gather.4.cloned.1.call-start = ((), (), s32[]{:S(2)}) async-start(), calls=%async_computation.4 | async-start | bytes 4718592 | tf_op jit(solution)/shard_map/all_gather | solution.py:128
  35.9 17.4 %copy-start.6 = (f32[2048]{0:T(1024)S(1)}, f32[2048]{0:T(1024)}, u32[]{:S(2)}) copy-start(f32[2048]{0:T(1024)} %param.29) | copy-start | bytes 24580
  50.6 4.7 copy-start.9
  53.1 30.1 %copy-start.13 = (bf16[2048,128]{1,0:T(8,128)(2,1)S(1)}, bf16[2048,128]{1,0:T(8,128)(2,1)}, u32[]{:S(2)}) copy-start(bf16[2048,128]{1,0:T(8,128)(2,1)} %param.32) | copy-start | bytes 1572868
  54.3 133.4 %reduce-scatter.3.cloned.1.call-start = ((), (), s32[]{:S(2)}) async-start(), calls=%async_computation.5 | async-start | bytes 9437184 | tf_op jit(solution)/shard_map/reduce_scatter | solution.py:171
  62.7 24.8 %copy-start.4 = (bf16[2048,128]{1,0:T(8,128)(2,1)S(1)}, bf16[2048,128]{1,0:T(8,128)(2,1)}, u32[]{:S(2)}) copy-start(bf16[2048,128]{1,0:T(8,128)(2,1)} %param.31) | copy-start | bytes 1572868
  83.2 4.4 copy-start.3
  86.8 2.3 copy-start.10
  86.8 3.7 copy-start.12
  90.5 4.8 copy-start.11
  95.3 2.5 copy-start.2
  102.4 15.9 %copy-start.5 = (bf16[1016,128]{1,0:T(8,128)(2,1)S(1)}, bf16[1016,128]{1,0:T(8,128)(2,1)}, u32[]{:S(2)}) copy-start(bf16[1016,128]{1,0:T(8,128)(2,1)} %slice.58) | copy-start | bytes 780292
  136.1 53.1 %copy-start.7 = (f32[2048]{0:T(1024)S(1)}, f32[2048]{0:T(1024)}, u32[]{:S(2)}) copy-start(f32[2048]{0:T(1024)} %param.36) | copy-start | bytes 24580
  136.1 125.4 %all-gather.6.cloned.1.call-start = ((), (), s32[]{:S(2)}) async-start(), calls=%async_computation.6 | async-start | bytes 8912896 | tf_op jit(solution)/shard_map/all_gather | solution.py:179
  190.1 207.0 %reduce-scatter.5.cloned.1.call-start = ((), (), s32[]{:S(2)}) async-start(), calls=%async_computation.7 | async-start | bytes 17825792 | tf_op jit(solution)/shard_map/reduce_scatter | solution.py:183
  287.0 115.3 %copy-start.8 = (f32[2048]{0:T(1024)S(1)}, f32[2048]{0:T(1024)}, u32[]{:S(2)}) copy-start(f32[2048]{0:T(1024)} %param.40) | copy-start | bytes 24580
  425.5 105.2 %all-to-all-start.1 = ((bf16[128,2,1024]{2,1,0:T(2,128)(2,1)}), bf16[128,2,1024]{2,1,0:T(2,128)(2,1)S(1)}, u32[]{:S(2)}, u32[]{:S(2)}) async-start(bf16[128,2,1024]{2,1,0:T(2,128)(2,1)} %reshape.486), calls=%async_computation.3 | async-start | bytes 1048576 | tf_op jit(solution)/shard_map/all_to_all | solution.py:77
Sparse Core Ops, SparseCore 0:
  10.8 4.6 sort.21.cloned.1.call-done
  54.4 28.7 all-gather.3
  136.2 51.3 reduce-scatter.2
  190.4 71.0 all-gather.5
  287.1 109.9 reduce-scatter.4
  (1 shorter events, 0.0 us)
where the time goes:
time: 545 us; the launch traced here: 540 us
  waiting for transfers between devices  266 us (49%)
  blocking collectives  114 us (21%)
  matrix products  74.9 us (14%)
  local copies, waits for them, and re-layouts  25.5 us (5%)
  other arithmetic  23.6 us (4%)
  starting transfers between devices  20.7 us (4%)
  between operations  15 us (3%)
    reduce_scatter x1, waiting for transfers between devices, shards(): lax.psum_scatter(jnp.dot(hidden_act, w_down, preferred_element_type=jnp.f...  110 us
    all_gather x1, waiting for transfers between devices, shards(): rows_piece = lax.all_gather(ffn_in, 'req', axis=0, tiled=True)  71.2 us
    pmax x1, blocking collectives, shards(): max_logit = lax.pmax(local_peaks, ('req', 'kv'))  68.8 us
    reduce_scatter x1, waiting for transfers between devices, shards(): lax.psum_scatter(jnp.dot(attended, o_proj, preferred_element_type=jnp.flo...  51.5 us
    psum x1, blocking collectives, spread(): return lax.psum(jnp.where(mine, value, jnp.zeros_like(value)), axis)  23.1 us
    all_gather x1, blocking collectives, shards(): lax.all_gather(tail_rows, 'req', axis=0, tiled=True)  22.4 us
    all_gather x1, waiting for transfers between devices, shards(): rows_piece = lax.all_gather(normed, 'kv', axis=0, tiled=True)  20.4 us
    all_to_all x2, starting transfers between devices, regroup(): lax.all_to_all(rows_in, ('req', 'kv'), split_axis=0, concat_axis=0, tiled...  20.1 us
  transfers between devices with their start and end apart: 6, of which 5 were waited for; matrix products, arithmetic and copies ran while one was open for 3% of the time, Pallas kernels for 0%

commit v1 on v0

--- a/solution.py
+++ b/solution.py
@@ -5,6 +5,14 @@
 
 EPS = 1e-06
 NEG = -1e30
+
+
+def gather_by_exchange(shard, axis, dim):
+    count = lax.axis_size(axis)
+    repeats = [count if d == dim else 1 for d in range(shard.ndim)]
+    return lax.all_to_all(
+        jnp.tile(shard, repeats), axis, split_axis=dim, concat_axis=dim, tiled=True
+    )
 
 
 def spread(value, axis, root):
@@ -176,7 +184,7 @@
     )
     resid = (owner_rows.astype(jnp.float32) + attn_part).astype(jnp.bfloat16)
     ffn_in = norm_rows(resid, ffn_gain).astype(jnp.bfloat16)
-    rows_piece = lax.all_gather(ffn_in, "req", axis=0, tiled=True)
+    rows_piece = gather_by_exchange(ffn_in, "req", 0)
     gate_part = jnp.dot(rows_piece, w_gate, preferred_element_type=jnp.float32)
     up_part = jnp.dot(rows_piece, w_up, preferred_element_type=jnp.float32)
     hidden_act = (jax.nn.silu(gate_part) * up_part).astype(jnp.bfloat16)

time: 545 us -> 574 us (1.053)
  blocking collectives: 114 us -> 216 us
  waiting for transfers between devices: 266 us -> 194 us
    all_to_all x0 -> x1, blocking collectives: none -> 102 us  [gather_by_exchange(): lax.all_to_all(jnp.tile(shard, repeats), axis, split_axis=dim, concat_axi...]
    all_gather x1 -> x0, waiting for transfers between devices: 71.2 us -> none  [shards(): rows_piece = lax.all_gather(ffn_in, 'req', axis=0, tiled=True)]
  transfers between devices with their start and end apart: 6 -> 5, of which waited for: 5 -> 4; matrix products, arithmetic and copies ran while one was open for 3% -> 2% of each run, Pallas kernels for 0% -> 0%
where the time goes in v1:
time: 574 us; the launch traced here: 570 us
  blocking collectives  216 us (38%)
  waiting for transfers between devices  194 us (34%)
  matrix products  70.9 us (12%)
  local copies, waits for them, and re-layouts  29.8 us (5%)
  other arithmetic  22.8 us (4%)
  starting transfers between devices  20.7 us (4%)
  between operations  15.1 us (3%)
    reduce_scatter x1, waiting for transfers between devices, shards(): lax.psum_scatter(jnp.dot(hidden_act, w_down, preferred_element_type=jnp.f...  109 us
    all_to_all x1, blocking collectives, gather_by_exchange(): lax.all_to_all(jnp.tile(shard, repeats), axis, split_axis=dim, concat_axi...  102 us
    pmax x1, blocking collectives, shards(): max_logit = lax.pmax(local_peaks, ('req', 'kv'))  68.8 us
    reduce_scatter x1, waiting for transfers between devices, shards(): lax.psum_scatter(jnp.dot(attended, o_proj, preferred_element_type=jnp.flo...  51.5 us
    psum x1, blocking collectives, spread(): return lax.psum(jnp.where(mine, value, jnp.zeros_like(value)), axis)  23.1 us
    all_gather x1, blocking collectives, shards(): lax.all_gather(tail_rows, 'req', axis=0, tiled=True)  22.4 us
    all_gather x1, waiting for transfers between devices, shards(): rows_piece = lax.all_gather(normed, 'kv', axis=0, tiled=True)  20.2 us
    all_to_all x2, starting transfers between devices, regroup(): lax.all_to_all(rows_in, ('req', 'kv'), split_axis=0, concat_axis=0, tiled...  20.1 us
  transfers between devices with their start and end apart: 5, of which 4 were waited for; matrix products, arithmetic and copies ran while one was open for 2% of the time, Pallas kernels for 0%

profile of v1, /device:TPU:1, one launch (start us, length us, event | category | flops | bytes accessed | tf_op | source)
XLA Modules:
  0.0 569.6 jit_solution(646262338270673463)
XLA Ops:
  11.1 4.7 sort.19.cloned.1.call-done
  23.6 11.5 %all-to-all-start = ((bf16[128,2,1024]{2,1,0:T(2,128)(2,1)}), bf16[128,2,1024]{2,1,0:T(2,128)(2,1)S(1)}, u32[]{:S(2)}, u32[]{:S(2)}) async-start(bf16[128,2,1024]{2,1,0:T(2,128)(2,1)} %reshape.491), calls=%async_computation | async-start | bytes 1048576 | tf_op jit(solution)/shard_map/all_to_all | solution.py:85
  35.9 13.0 %all-to-all-done = bf16[128,2,1024]{2,1,0:T(2,128)(2,1)S(1)} async-done(((bf16[128,2,1024]{2,1,0:T(2,128)(2,1)}), bf16[128,2,1024]{2,1,0:T(2,128)(2,1)S(1)}, u32[]{:S(2)}, u32[]{:S(2)}) %all-to-all-start) | async-done | bytes 524320 | tf_op jit(solution)/shard_map/all_to_all | solution.py:85
  55.6 3.1 multiply_cosine_fusion
  58.8 4.2 fusion.4
  63.0 20.2 %all-gather.3.cloned.1.call-done = bf16[1024,2048]{1,0:T(8,128)(2,1)} async-done(((bf16[128,2048]{1,0:T(8,128)(2,1)}), bf16[1024,2048]{1,0:T(8,128)(2,1)}) %all-gather.3.cloned.1.call-update) | async-done | bytes 4194320 | tf_op jit(solution)/shard_map/all_gather | solution.py:136
  83.2 3.6 convolution_convert_fusion
  90.5 2.3 multiply_reduce_fusion
  99.5 2.9 fusion.43
  102.4 15.5 %fusion.84 = (f32[2,1016]{1,0:T(2,128)S(1)}, f32[2,1016,3064]{2,1,0:T(8,128)}) fusion(pred[1016,3064]{1,0:T(8,128)(4,1)} %fusion.4, bf16[1016,128]{1,0:T(8,128)(2,1)} %copy.80, bf16[2048,128]{1,0:T(8,128)(2,1)} %bitcast.108, bf16[1024,2,64]{2,0,1:T(8,128)(2,1)S(1)} %get-tuple-element.6, bf16[1024,2,64]{2,0,1:T(8,128)(2,1)S(1)} %get-tuple-element.7), kind=kOutput, calls=%fused_computation.161 | convolution fusion | flops 1621384704 | bytes 29334016 | tf_op jit(solution)/shard_map/sub | solution.py:56
  118.0 11.7 %fusion.12 = bf16[1016,2,128]{2,0,1:T(8,128)(2,1)S(1)} fusion(f32[2,1016,3064]{2,1,0:T(8,128)} %get-tuple-element.21, f32[2,1016]{1,0:T(2,128)S(1)} %get-tuple-element.20, bf16[1016,128]{1,0:T(8,128)(2,1)S(1)} %copy-done.6, bf16[2048,128]{1,0:T(8,128)(2,1)} %bitcast.109), kind=kOutput, calls=%fused_computation.28 | convolution fusion | flops 1608149248 | bytes 26216896 | tf_op jit(solution)/shard_map/gck,kd->cgd/dot_general | solution.py:58
  130.0 5.7 %fusion.89 = f32[1024,2048]{1,0:T(8,128)} fusion(bf16[1024,256]{0,1:T(8,128)(2,1)S(1)} %bitcast.97, bf16[256,2048]{1,0:T(8,128)(2,1)} %param.35), kind=kOutput, calls=%fused_computation.162 | convolution fusion | flops 1073741824 | bytes 9961472 | tf_op jit(solution)/shard_map/dot_general | solution.py:180
  135.8 51.5 %reduce-scatter.3.cloned.1.call-done = f32[128,2048]{1,0:T(8,128)} async-done(((f32[1024,2048]{1,0:T(8,128)}), f32[128,2048]{1,0:T(8,128)}) %reduce-scatter.3.cloned.1.call-update) | async-done | bytes 1048592 | tf_op jit(solution)/shard_map/reduce_scatter | solution.py:179
  190.0 101.9 %all_to_all.33 = bf16[16,128,2048]{2,1,0:T(8,128)(2,1)S(1)} all-to-all(bf16[16,128,2048]{2,1,0:T(8,128)(2,1)S(1)} %tile.2), channel_id=1, replica_groups=mesh['req'=16,'kv'=8] {'req'}, dimensions={0} | all-to-all | bytes 16777216 | tf_op jit(solution)/shard_map/all_to_all | solution.py:13
  291.9 3.2 copy-done.2
  295.1 6.4 %fusion.90 = f32[2048,384]{1,0:T(8,128)} fusion(bf16[2048,2048]{1,0:T(8,128)(2,1)S(1)} %bitcast.92, bf16[2048,384]{1,0:T(8,128)(2,1)S(1)} %copy-done.13), kind=kOutput, calls=%fused_computation.163 | convolution fusion | flops 3221225472 | bytes 13107200 | tf_op jit(solution)/shard_map/dot_general | solution.py:188
  301.6 15.4 %fusion.10 = f32[2048,2048]{1,0:T(8,128)} fusion(bf16[384,2048]{1,0:T(8,128)(2,1)S(1)} %copy-done, f32[2048,384]{1,0:T(8,128)} %fusion.90, bf16[2048,2048]{1,0:T(8,128)(2,1)} %bitcast.93, bf16[2048,384]{1,0:T(8,128)(2,1)} %param.38), kind=kOutput, calls=%fused_computation.26 | convolution fusion | flops 6447169536 | bytes 31457280 | tf_op jit(solution)/shard_map/dot_general | solution.py:192
  317.0 109.3 %reduce-scatter.5.cloned.1.call-done = f32[128,2048]{1,0:T(8,128)} async-done(((f32[2048,2048]{1,0:T(8,128)}), f32[128,2048]{1,0:T(8,128)}) %reduce-scatter.5.cloned.1.call-update) | async-done | bytes 1048592 | tf_op jit(solution)/shard_map/reduce_scatter | solution.py:191
  431.6 23.1 %psum.7 = bf16[9,2048]{1,0:T(8,128)(2,1)S(1)} all-reduce(bf16[9,2048]{1,0:T(8,128)(2,1)S(1)} %fusion.48), channel_id=1, replica_groups=mesh['req'=16,'kv'=8] {'kv'}, use_global_device_ids=true, to_apply=%region_16.17 | all-reduce | flops 18432 | bytes 73728 | tf_op jit(solution)/shard_map/psum | solution.py:20
  454.7 8.6 %all-to-all-start.2 = ((bf16[128,2,1024]{2,1,0:T(2,128)(2,1)}), bf16[128,2,1024]{2,1,0:T(2,128)(2,1)S(1)}, u32[]{:S(2)}, u32[]{:S(2)}) async-start(bf16[128,2,1024]{2,1,0:T(2,128)(2,1)} %reshape.493), calls=%async_computation.4 | async-start | bytes 1048576 | tf_op jit(solution)/shard_map/all_to_all | solution.py:85
  463.3 22.4 %all-gather = bf16[16,9,2048]{2,1,0:T(8,128)(2,1)S(1)} all-gather(bf16[1,9,2048]{2,1,0:T(8,128)(2,1)S(1)} %bitcast.102), channel_id=1, replica_groups=mesh['req'=16,'kv'=8] {'req'}, dimensions={0}, use_global_device_ids=true | all-gather | bytes 626688 | tf_op jit(solution)/shard_map/all_gather | solution.py:205
  486.7 4.4 convolution_reduce_fusion
  491.1 68.8 %pmax.7 = f32[144]{0:T(256)} all-reduce(f32[144]{0:T(256)S(1)} %convolution_reduce_fusion), channel_id=1, replica_groups=mesh['req'=16,'kv'=8] {'req','kv'}, use_global_device_ids=true, to_apply=%region_18.19 | all-reduce | flops 144 | bytes 1152 | tf_op jit(solution)/shard_map/pmax | solution.py:211
  560.4 2.4 scatter_custom_fusion.1
  (113 shorter events, 38.8 us)
Async XLA Ops:
  7.2 294.4 %copy-start = (bf16[384,2048]{1,0:T(8,128)(2,1)S(1)}, bf16[384,2048]{1,0:T(8,128)(2,1)}, u32[]{:S(2)}) copy-start(bf16[384,2048]{1,0:T(8,128)(2,1)} %param.39) | copy-start | bytes 4718596
  7.2 12.8 %copy-start.1 = (bf16[128,2048]{1,0:T(8,128)(2,1)S(1)}, bf16[128,2048]{1,0:T(8,128)(2,1)}, u32[]{:S(2)}) copy-start(bf16[128,2048]{1,0:T(8,128)(2,1)} %param.21) | copy-start | bytes 1572868
  7.2 8.5 %sort.19.cloned.1.call-start = ((), (), s32[]{:S(2)}) async-start(), calls=%async_computation.8 | async-start | bytes 393248 | tf_op jit(solution)/shard_map/jit(argsort)/sort | solution.py:119
  23.6 25.2 %all-to-all-start = ((bf16[128,2,1024]{2,1,0:T(2,128)(2,1)}), bf16[128,2,1024]{2,1,0:T(2,128)(2,1)S(1)}, u32[]{:S(2)}, u32[]{:S(2)}) async-start(bf16[128,2,1024]{2,1,0:T(2,128)(2,1)} %reshape.491), calls=%async_computation | async-start | bytes 1048576 | tf_op jit(solution)/shard_map/all_to_all | solution.py:85
  35.1 48.0 %all-gather.3.cloned.1.call-start = ((), (), s32[]{:S(2)}) async-start(), calls=%async_computation.5 | async-start | bytes 4718592 | tf_op jit(solution)/shard_map/all_gather | solution.py:136
  35.9 17.4 %copy-start.7 = (f32[2048]{0:T(1024)S(1)}, f32[2048]{0:T(1024)}, u32[]{:S(2)}) copy-start(f32[2048]{0:T(1024)} %param.29) | copy-start | bytes 24580
  50.6 5.0 copy-start.10
  53.1 30.1 %copy-start.15 = (bf16[2048,128]{1,0:T(8,128)(2,1)S(1)}, bf16[2048,128]{1,0:T(8,128)(2,1)}, u32[]{:S(2)}) copy-start(bf16[2048,128]{1,0:T(8,128)(2,1)} %param.32) | copy-start | bytes 1572868
  54.3 133.0 %reduce-scatter.3.cloned.1.call-start = ((), (), s32[]{:S(2)}) async-start(), calls=%async_computation.6 | async-start | bytes 9437184 | tf_op jit(solution)/shard_map/reduce_scatter | solution.py:179
  63.0 24.6 %copy-start.5 = (bf16[2048,128]{1,0:T(8,128)(2,1)S(1)}, bf16[2048,128]{1,0:T(8,128)(2,1)}, u32[]{:S(2)}) copy-start(bf16[2048,128]{1,0:T(8,128)(2,1)} %param.31) | copy-start | bytes 1572868
  83.2 4.4 copy-start.4
  86.8 2.3 copy-start.11
  86.8 3.7 copy-start.14
  90.5 4.8 copy-start.12
  95.3 2.5 copy-start.3
  102.4 15.5 %copy-start.6 = (bf16[1016,128]{1,0:T(8,128)(2,1)S(1)}, bf16[1016,128]{1,0:T(8,128)(2,1)}, u32[]{:S(2)}) copy-start(bf16[1016,128]{1,0:T(8,128)(2,1)} %slice.58) | copy-start | bytes 780292
  135.7 53.0 %copy-start.8 = (f32[2048]{0:T(1024)S(1)}, f32[2048]{0:T(1024)}, u32[]{:S(2)}) copy-start(f32[2048]{0:T(1024)} %param.36) | copy-start | bytes 24580
  135.7 290.6 %reduce-scatter.5.cloned.1.call-start = ((), (), s32[]{:S(2)}) async-start(), calls=%async_computation.7 | async-start | bytes 17825792 | tf_op jit(solution)/shard_map/reduce_scatter | solution.py:191
  190.0 105.1 %copy-start.13 = (bf16[2048,384]{1,0:T(8,128)(2,1)S(1)}, bf16[2048,384]{1,0:T(8,128)(2,1)}, u32[]{:S(2)}) copy-start(bf16[2048,384]{1,0:T(8,128)(2,1)} %param.37) | copy-start | bytes 4718596
  291.9 3.2 copy-start.2
  317.0 114.5 %copy-start.9 = (f32[2048]{0:T(1024)S(1)}, f32[2048]{0:T(1024)}, u32[]{:S(2)}) copy-start(f32[2048]{0:T(1024)} %param.40) | copy-start | bytes 24580
  454.7 105.2 %all-to-all-start.2 = ((bf16[128,2,1024]{2,1,0:T(2,128)(2,1)}), bf16[128,2,1024]{2,1,0:T(2,128)(2,1)S(1)}, u32[]{:S(2)}, u32[]{:S(2)}) async-start(bf16[128,2,1024]{2,1,0:T(2,128)(2,1)} %reshape.493), calls=%async_computation.4 | async-start | bytes 1048576 | tf_op jit(solution)/shard_map/all_to_all | solution.py:85
Sparse Core Ops, SparseCore 0:
  10.8 4.6 sort.21.cloned.1.call-done
  54.4 28.7 all-gather.2
  135.9 51.3 reduce-scatter.2
  317.1 109.1 reduce-scatter.4
  (1 shorter events, 0.0 us)
